TPU v7x, 32 devices: a whole 2x2x4 slice. The times are simulated.
32 devices in a mesh: groups: 2 (over x), dp: 16 (over z, y, core).
Axes of the slice: x: 2, y: 2, z: 4, core: 2. Of those that a mesh axis runs over, the one named last changes fastest.
Arguments:
- activations: bfloat16 [12288, 16384], P(('groups', 'dp')), parts along dimension 0, may hold values from -18 to 18
- labels: int32 [12288], P(('groups', 'dp')), parts along dimension 0, may hold values from 0 to 63, as said below
- counts: int32 [12288], P(('groups', 'dp')), parts along dimension 0, may hold values from 1 to 4
Outputs:
- solution: float32 [32768, 64], P(('groups', 'dp')), parts along dimension 0
- residual: float32 [32768, 64], P(('groups', 'dp')), parts along dimension 0
There are 2 independent parts, one for each index of `groups`. A program takes and returns all parts, laid end to end along the dimension named above; each array names one. Nothing has to cross between parts.
Inputs may be any that keep to these rules, and one draw needn't show every extreme that they name: `labels`: concept index of each row; every concept of 0 to 63 names at least one row. `counts`: integer sample weight of each row.
All inputs are finite; a program needn't handle non-finite values.
Results may differ from a plain program's by a relative error of at most 0.012.
The roundings to bfloat16 on the way count: a program that leaves them out, or rounds other values in their place, can miss the bound.
Values may be sent and summed in bfloat16 or wider, within the bound.
No kernel may reach another device: no remote copies, remote signals or barrier semaphores. Data moves between devices by JAX's collectives and lax.ppermute only.
A program may use at most 64 MiB of HBM per device.

v0:
```python
import jax
import jax.numpy as jnp
from jax import lax
from jax.sharding import PartitionSpec as P

K = 64
ITERS = 2
RIDGE = 0.1


def precise(left_side, right_side):
    return jnp.dot(
        left_side, right_side, precision=lax.Precision.HIGHEST, preferred_element_type=jnp.float32
    )


def symmetric(matrix):
    return 0.5 * (matrix + matrix.T)


def solve_positive(matrix, target):
    return jax.scipy.linalg.cho_solve((jnp.linalg.cholesky(matrix), True), target)


def contract_rows(left_side, right_side):
    return lax.dot_general(
        left_side, right_side, (((0,), (0,)), ((), ())), preferred_element_type=jnp.float32
    )


def per_device(activations, labels, counts):
    weights = counts.astype(jnp.float32)
    classes = jnp.arange(K, dtype=jnp.int32)
    member_full = jnp.where(labels[:, None] == classes[None, :], weights[:, None], jnp.float32(0.0))
    local_weight = jnp.sum(member_full, axis=0)
    member = member_full.astype(jnp.bfloat16)
    class_sums = lax.psum_scatter(
        contract_rows(activations, member), "dp", scatter_dimension=0, tiled=True
    )
    class_weight = lax.psum(local_weight, "dp")
    total_weight = jnp.sum(class_weight)
    class_means = class_sums / class_weight[None, :]
    mean_diff = class_means * jnp.sqrt(class_weight)[None, :]
    solution = jnp.zeros_like(mean_diff)
    residual = mean_diff
    direction = mean_diff
    current = symmetric(lax.psum(precise(residual.T, residual), "dp"))
    for iteration in range(ITERS):
        probed = jnp.dot(
            activations,
            lax.all_gather(direction.astype(jnp.bfloat16), "dp", axis=0, tiled=True),
            preferred_element_type=jnp.float32,
        )
        weighted = (weights[:, None] * probed).astype(jnp.bfloat16)
        panel = lax.psum_scatter(
            contract_rows(activations, weighted), "dp", scatter_dimension=0, tiled=True
        )
        cross, along_panel, along_along = lax.psum(
            (
                precise(class_means.T, direction),
                precise(direction.T, panel),
                precise(direction.T, direction),
            ),
            "dp",
        )
        scaled = class_weight[:, None] * cross
        curvature = symmetric(
            (along_panel - precise(cross.T, scaled)) / total_weight + RIDGE * along_along
        )
        step_alpha = solve_positive(curvature, current)
        image = (panel - precise(class_means, scaled)) / total_weight + RIDGE * direction
        solution = solution + precise(direction, step_alpha)
        residual = residual - precise(image, step_alpha)
        renewed = current
        if iteration + 1 < ITERS:
            renewed = symmetric(lax.psum(precise(residual.T, residual), "dp"))
        if iteration + 1 < ITERS:
            step_beta = solve_positive(current, renewed)
            direction = residual + precise(direction, step_beta)
            current = renewed
    return (solution, residual)


def solution(mesh):
    in_specs = (P(("groups", "dp"), None), P(("groups", "dp")), P(("groups", "dp")))
    out_specs = (P(("groups", "dp"), None), P(("groups", "dp"), None))
    return jax.shard_map(
        per_device, mesh=mesh, in_specs=in_specs, out_specs=out_specs, check_vma=False
    )
```

profile of v0, /device:TPU:0, one launch (start us, length us, event | category | flops | bytes accessed | tf_op | source)
XLA Modules:
  0.0 587.8 jit_solution(6999212861251710433)
XLA Ops:
  7.2 0.7 convert_element_type.20
  7.9 8.9 %convolution_bitcast_fusion.2 = f32[16384,64]{0,1:T(8,128)} fusion(bf16[384,16384]{1,0:T(8,128)(2,1)} %param.6, f32[384]{0:T(512)S(1)} %convert_element_type.20, s32[384]{0:T(512)} %param.7), kind=kOutput, calls=%fused_computation.2 | convolution fusion | flops 805355520 | bytes 16780288 | tf_op jit(solution)/shard_map/dot_general | solution.py:26
  17.0 35.0 %psum.59 = f32[64]{0:T(128)S(1)} all-reduce(f32[64]{0:T(128)S(1)} %select_reduce_fusion), channel_id=1, replica_groups=mesh['groups'=2,'dp'=16] {'dp'}, use_global_device_ids=true, to_apply=%region_2.3 | all-reduce | flops 64 | bytes 512 | tf_op jit(solution)/shard_map/psum | solution.py:40
  52.0 0.6 fusion.62
  52.6 39.5 %reduce-scatter.4.cloned.1.call-done = f32[1024,64]{0,1:T(8,128)} async-done(((f32[16384,64]{0,1:T(8,128)}), f32[1024,64]{0,1:T(8,128)}) %reduce-scatter.4.cloned.1.call-update) | async-done | bytes 262160 | tf_op jit(solution)/shard_map/reduce_scatter | solution.py:37
  92.1 1.7 multiply_convert_fusion
  93.9 41.7 %all-gather.3.cloned.1.call-done = bf16[16384,64]{0,1:T(8,128)(2,1)} async-done(((bf16[1024,64]{0,1:T(8,128)(2,1)}), bf16[16384,64]{0,1:T(8,128)(2,1)}) %all-gather.3.cloned.1.call-update) | async-done | bytes 2097168 | tf_op jit(solution)/shard_map/all_gather | solution.py:51
  135.5 18.5 %convolution_bitcast_fusion.1 = f32[16384,64]{0,1:T(8,128)} fusion(bf16[384,16384]{1,0:T(8,128)(2,1)} %param.6, bf16[16384,64]{0,1:T(8,128)(2,1)} %all-gather.3.cloned.1.call-done, f32[384]{0:T(512)S(1)} %convert_element_type.20), kind=kOutput, calls=%fused_computation.1 | convolution fusion | flops 1610661888 | bytes 18875904 | tf_op jit(solution)/shard_map/dot_general | solution.py:26
  154.1 0.5 fusion.13
  154.5 0.5 fusion.15
  155.0 70.3 %reduce-scatter.6.cloned.1.call-done = f32[1024,64]{0,1:T(8,128)} async-done(((f32[16384,64]{0,1:T(8,128)}), f32[1024,64]{0,1:T(8,128)}) %reduce-scatter.6.cloned.1.call-update) | async-done | bytes 262160 | tf_op jit(solution)/shard_map/reduce_scatter | solution.py:55
  225.3 1.4 fusion.17
  226.7 59.2 %all-reduce.1 = (f32[64,64]{1,0:T(8,128)S(1)}, f32[64,64]{1,0:T(8,128)S(1)}, f32[64,64]{1,0:T(8,128)S(1)}) all-reduce(f32[64,64]{1,0:T(8,128)S(1)} %fusion.13, f32[64,64]{1,0:T(8,128)S(1)} %fusion.17, f32[64,64]{1,0:T(8,128)S(1)} %fusion.15), channel_id=1, replica_groups=mesh['groups'=2,'dp'=16] {'dp'}, use_global_device_ids=true, to_apply=%region_7.8 | all-reduce | flops 12288 | bytes 98304 | tf_op jit(solution)/shard_map/psum | solution.py:58
  286.1 5.8 cholesky.70
  292.0 0.6 compare_reduce_fusion.1
  292.6 0.7 fusion.32
  293.3 4.9 custom-call.10
  298.2 0.9 fusion.9
  299.4 5.9 cholesky.59
  305.3 0.6 compare_reduce_fusion.2
  305.9 0.7 fusion.31
  306.6 4.9 custom-call.9
  311.5 0.2 fusion.48
  311.9 2.1 fusion.3
  314.0 0.4 convolution_subtract_fusion.2
  314.4 0.4 fusion.64
  314.8 57.6 %psum.63 = f32[64,64]{1,0:T(8,128)S(1)} all-reduce(f32[64,64]{1,0:T(8,128)S(1)} %fusion.64), channel_id=1, replica_groups=mesh['groups'=2,'dp'=16] {'dp'}, use_global_device_ids=true, to_apply=%region_10.13 | all-reduce | flops 4096 | bytes 32768 | tf_op jit(solution)/shard_map/psum | solution.py:76
  372.5 0.2 fusion.42
  372.8 0.2 fusion.40
  372.9 1.1 fusion.63
  374.1 0.3 reduce-scatter.8.cloned.1.call-start
  374.3 38.6 %all-gather.5.cloned.1.call-done = bf16[16384,64]{0,1:T(8,128)(2,1)} async-done(((bf16[1024,64]{0,1:T(8,128)(2,1)}), bf16[16384,64]{0,1:T(8,128)(2,1)}) %all-gather.5.cloned.1.call-update) | async-done | bytes 2097168 | tf_op jit(solution)/shard_map/all_gather | solution.py:51
  412.9 18.5 %convolution_bitcast_fusion = f32[16384,64]{0,1:T(8,128)} fusion(bf16[384,16384]{1,0:T(8,128)(2,1)} %param.6, bf16[16384,64]{0,1:T(8,128)(2,1)} %all-gather.5.cloned.1.call-done, f32[384]{0:T(512)S(1)} %convert_element_type.20), kind=kOutput, calls=%fused_computation | convolution fusion | flops 1610661888 | bytes 18875904 | tf_op jit(solution)/shard_map/dot_general | solution.py:26
  431.4 0.4 fusion.66
  431.7 0.4 fusion.61
  432.2 0.5 fusion.11
  432.6 70.1 %reduce-scatter.8.cloned.1.call-done = f32[1024,64]{0,1:T(8,128)} async-done(((f32[16384,64]{0,1:T(8,128)}), f32[1024,64]{0,1:T(8,128)}) %reduce-scatter.8.cloned.1.call-update) | async-done | bytes 262160 | tf_op jit(solution)/shard_map/reduce_scatter | solution.py:55
  502.8 1.3 fusion.65
  504.1 59.1 %all-reduce = (f32[64,64]{1,0:T(8,128)S(1)}, f32[64,64]{1,0:T(8,128)S(1)}, f32[64,64]{1,0:T(8,128)S(1)}) all-reduce(f32[64,64]{1,0:T(8,128)S(1)} %fusion.65, f32[64,64]{1,0:T(8,128)S(1)} %fusion.61, f32[64,64]{1,0:T(8,128)S(1)} %fusion.66), channel_id=1, replica_groups=mesh['groups'=2,'dp'=16] {'dp'}, use_global_device_ids=true, to_apply=%region_12.15 | all-reduce | flops 12288 | bytes 98304 | tf_op jit(solution)/shard_map/psum | solution.py:58
  563.2 0.9 fusion.7
  564.4 5.8 cholesky.81
  570.3 0.6 compare_reduce_fusion
  570.9 0.7 fusion.33
  571.6 4.9 custom-call.11
  576.5 0.2 fusion.36
  576.9 2.1 fusion.1
  579.0 1.1 convolution_subtract_fusion
  580.1 1.1 convolution_add_fusion
  (35 shorter events, 1.5 us)
Async XLA Ops:
  7.2 9.7 %copy-start.1 = (s32[384]{0:T(512)S(1)}, s32[384]{0:T(512)}, u32[]{:S(2)}) copy-start(s32[384]{0:T(512)} %param.7) | copy-start | bytes 4612
  7.2 84.9 %reduce-scatter.4.cloned.1.call-start = ((), (), s32[]{:S(2)}) async-start(), calls=%async_computation.3 | async-start | bytes 4456448 | tf_op jit(solution)/shard_map/reduce_scatter | solution.py:37
  16.8 118.7 %all-gather.3.cloned.1.call-start = ((), (), s32[]{:S(2)}) async-start(), calls=%async_computation.4 | async-start | bytes 2228224 | tf_op jit(solution)/shard_map/all_gather | solution.py:51
  93.8 60.3 %copy-start = (f32[1024,64]{0,1:T(8,128)S(1)}, f32[1024,64]{0,1:T(8,128)}, u32[]{:S(2)}) copy-start(f32[1024,64]{0,1:T(8,128)} %reduce-scatter.4.cloned.1.call-done) | copy-start | bytes 786436
  93.8 131.5 %reduce-scatter.6.cloned.1.call-start = ((), (), s32[]{:S(2)}) async-start(), calls=%async_computation.5 | async-start | bytes 4456448 | tf_op jit(solution)/shard_map/reduce_scatter | solution.py:55
  154.0 258.9 %all-gather.5.cloned.1.call-start = ((), (), s32[]{:S(2)}) async-start(), calls=%async_computation.6 | async-start | bytes 2228224 | tf_op jit(solution)/shard_map/all_gather | solution.py:51
  374.1 128.7 %reduce-scatter.8.cloned.1.call-start = ((), (), s32[]{:S(2)}) async-start(), calls=%async_computation.7 | async-start | bytes 4456448 | tf_op jit(solution)/shard_map/reduce_scatter | solution.py:55
Sparse Core Ops, SparseCore 0:
  16.9 75.1 reduce-scatter.3
  95.1 40.4 all-gather.2
  154.1 71.1 reduce-scatter.5
  374.2 38.6 all-gather.4
  431.5 71.2 reduce-scatter.7
where the time goes:
time: 588 us
  waiting for transfers between devices  260 us (44%)
  blocking collectives  211 us (36%)
  matrix products  62 us (11%)
  other arithmetic  39.4 us (7%)
  between operations  14.1 us (2%)
    reduce_scatter x2, waiting for transfers between devices, per_device(): lax.psum_scatter(contract_rows(activations, weighted), 'dp', scatter_dime...  140 us
    psum x2, blocking collectives, per_device(): lax.psum((precise(class_means.T, direction), precise(direction.T, panel),...  118 us
    all_gather x2, waiting for transfers between devices, per_device(): lax.all_gather(direction.astype(jnp.bfloat16), 'dp', axis=0, tiled=True)  80.2 us
    psum x1, blocking collectives, per_device(): renewed = symmetric(lax.psum(precise(residual.T, residual), 'dp'))  57.6 us
    dot_general x3, matrix products, contract_rows(): lax.dot_general(left_side, right_side, (((0,), (0,)), ((), ())), preferre...  45.8 us
    reduce_scatter x1, waiting for transfers between devices, per_device(): lax.psum_scatter(contract_rows(activations, member), 'dp', scatter_dimens...  39.5 us
    psum x1, blocking collectives, per_device(): class_weight = lax.psum(local_weight, 'dp')  35 us
    another operation x9, other arithmetic, solve_positive(): jnp.linalg.cholesky(matrix)  19.6 us
  transfers between devices with their start and end apart: 5, of which 5 were waited for; matrix products, arithmetic and copies ran while one was open for 0% of the time, Pallas kernels for 0%

commit v1 on v0

--- a/solution.py
+++ b/solution.py
@@ -46,9 +46,39 @@
     direction = mean_diff
     current = symmetric(lax.psum(precise(residual.T, residual), "dp"))
     for iteration in range(ITERS):
+
+        def note_sides(sample):
+            g_now = lax.psum(1, "dp")
+            p_next, e_next, all_rows = (g_now, lax.axis_index("dp"), sample.shape[0])
+            top = latest = sample
+            w = 1
+            y_new = lax.dynamic_update_slice_in_dim(
+                jnp.zeros(
+                    tuple((kk * p_next if q == 0 else kk for q, kk in enumerate(sample.shape))),
+                    sample.dtype,
+                ),
+                sample,
+                e_next * all_rows,
+                axis=0,
+            )
+            while w < p_next // 2 + 1:
+                top = lax.ppermute(top, "dp", tuple(((q, (q + 1) % p_next) for q in range(p_next))))
+                y_new = lax.dynamic_update_slice_in_dim(
+                    y_new, top, (e_next - w) % p_next * all_rows, axis=0
+                )
+                if 2 * w < p_next:
+                    latest = lax.ppermute(
+                        latest, "dp", tuple(((q, (q - 1) % p_next) for q in range(p_next)))
+                    )
+                    y_new = lax.dynamic_update_slice_in_dim(
+                        y_new, latest, (e_next + w) % p_next * all_rows, axis=0
+                    )
+                w += 1
+            return y_new
+
         probed = jnp.dot(
             activations,
-            lax.all_gather(direction.astype(jnp.bfloat16), "dp", axis=0, tiled=True),
+            note_sides(direction.astype(jnp.bfloat16)),
             preferred_element_type=jnp.float32,
         )
         weighted = (weights[:, None] * probed).astype(jnp.bfloat16)

time: 588 us -> 616 us (1.048)
  starting transfers between devices: 0.43 us -> 62.8 us
  waiting for transfers between devices: 260 us -> 228 us
    all_gather x2 -> x0, waiting for transfers between devices: 80.2 us -> none  [per_device(): lax.all_gather(direction.astype(jnp.bfloat16), 'dp', axis=0, tiled=True)]
    ppermute x0 -> x30, starting transfers between devices: none -> 62.7 us  [the longest x14 62.6 us: note_sides(): lax.ppermute(latest, 'dp', tuple(((q, (q - 1) % p_next) for q in range(p_...]
    ppermute x0 -> x30, waiting for transfers between devices: none -> 51.4 us  [the longest x16 51.3 us: note_sides(): lax.ppermute(top, 'dp', tuple(((q, (q + 1) % p_next) for q in range(p_nex...]
  transfers between devices with their start and end apart: 5 -> 33, of which waited for: 5 -> 19; matrix products, arithmetic and copies ran while one was open for 0% -> 1% of each run, Pallas kernels for 0% -> 0%
where the time goes in v1:
time: 616 us
  waiting for transfers between devices  228 us (37%)
  blocking collectives  211 us (34%)
  starting transfers between devices  62.8 us (10%)
  matrix products  59.2 us (10%)
  other arithmetic  37.8 us (6%)
  between operations  14.3 us (2%)
    reduce_scatter x2, waiting for transfers between devices, per_device(): lax.psum_scatter(contract_rows(activations, weighted), 'dp', scatter_dime...  138 us
    psum x2, blocking collectives, per_device(): lax.psum((precise(class_means.T, direction), precise(direction.T, panel),...  118 us
    ppermute x14, starting transfers between devices, note_sides(): lax.ppermute(latest, 'dp', tuple(((q, (q - 1) % p_next) for q in range(p_...  62.6 us
    psum x1, blocking collectives, per_device(): renewed = symmetric(lax.psum(precise(residual.T, residual), 'dp'))  57.6 us
    ppermute x16, waiting for transfers between devices, note_sides(): lax.ppermute(top, 'dp', tuple(((q, (q + 1) % p_next) for q in range(p_nex...  51.3 us
    dot_general x3, matrix products, contract_rows(): lax.dot_general(left_side, right_side, (((0,), (0,)), ((), ())), preferre...  44.5 us
    reduce_scatter x1, waiting for transfers between devices, per_device(): lax.psum_scatter(contract_rows(activations, member), 'dp', scatter_dimens...  38.9 us
    psum x1, blocking collectives, per_device(): class_weight = lax.psum(local_weight, 'dp')  35 us
  transfers between devices with their start and end apart: 33, of which 19 were waited for; matrix products, arithmetic and copies ran while one was open for 1% of the time, Pallas kernels for 0%

profile of v1, /device:TPU:0, one launch (start us, length us, event | category | flops | bytes accessed | tf_op | source)
XLA Modules:
  0.0 615.6 jit_solution(14897720237163149309)
XLA Ops:
  7.9 8.9 %convolution_bitcast_fusion.2 = f32[16384,64]{0,1:T(8,128)} fusion(bf16[384,16384]{1,0:T(8,128)(2,1)} %param.6, f32[384]{0:T(512)S(1)} %convert_element_type.20, s32[384]{0:T(512)} %param.7), kind=kOutput, calls=%fused_computation.2 | convolution fusion | flops 805355520 | bytes 16780288 | tf_op jit(solution)/shard_map/dot_general | solution.py:26
  17.5 35.0 %psum.59 = f32[64]{0:T(128)S(1)} all-reduce(f32[64]{0:T(128)S(1)} %select_reduce_fusion), channel_id=1, replica_groups=mesh['groups'=2,'dp'=16] {'dp'}, use_global_device_ids=true, to_apply=%region_2.3 | all-reduce | flops 64 | bytes 512 | tf_op jit(solution)/shard_map/psum | solution.py:40
  53.2 38.9 %reduce-scatter.4.cloned.1.call-done = f32[1024,64]{0,1:T(8,128)} async-done(((f32[16384,64]{0,1:T(8,128)}), f32[1024,64]{0,1:T(8,128)}) %reduce-scatter.4.cloned.1.call-update) | async-done | bytes 262160 | tf_op jit(solution)/shard_map/reduce_scatter | solution.py:37
  93.2 4.4 collective-permute-start.1
  97.6 2.6 collective-permute-done
  100.3 4.5 collective-permute-start.3
  104.9 2.6 collective-permute-done.2
  107.5 4.4 collective-permute-start.5
  111.9 2.7 collective-permute-done.4
  114.7 4.4 collective-permute-start.7
  119.1 2.7 collective-permute-done.6
  121.9 4.4 collective-permute-start.9
  126.3 2.7 collective-permute-done.8
  129.1 4.4 collective-permute-start.11
  133.5 2.7 collective-permute-done.10
  136.3 4.4 collective-permute-start.13
  140.7 2.6 collective-permute-done.12
  143.4 7.0 %collective-permute-done.14 = bf16[1024,64]{0,1:T(8,128)(2,1)S(1)} collective-permute-done((bf16[1024,64]{0,1:T(8,128)(2,1)S(1)}, bf16[1024,64]{0,1:T(8,128)(2,1)S(1)}, u32[]{:S(2)}, u32[]{:S(2)}) %collective-permute-start.14) | collective-permute-done | bytes 131104 | tf_op jit(solution)/shard_map/ppermute | solution.py:65
  150.4 17.8 %convolution_bitcast_fusion.1 = f32[16384,64]{0,1:T(8,128)} fusion(bf16[384,16384]{1,0:T(8,128)(2,1)} %param.6, bf16[16384,64]{0,1:T(8,128)(2,1)S(1)} %constant_dynamic-update-slice_fusion.16, f32[384]{0:T(512)S(1)} %convert_element_type.20), kind=kOutput, calls=%fused_computation.1 | convolution fusion | flops 1610661888 | bytes 18875904 | tf_op jit(solution)/shard_map/dot_general | solution.py:26
  169.3 68.7 %reduce-scatter.6.cloned.1.call-done = f32[1024,64]{0,1:T(8,128)} async-done(((f32[16384,64]{0,1:T(8,128)}), f32[1024,64]{0,1:T(8,128)}) %reduce-scatter.6.cloned.1.call-update) | async-done | bytes 262160 | tf_op jit(solution)/shard_map/reduce_scatter | solution.py:85
  238.0 1.4 fusion.17
  239.5 59.2 %all-reduce.1 = (f32[64,64]{1,0:T(8,128)S(1)}, f32[64,64]{1,0:T(8,128)S(1)}, f32[64,64]{1,0:T(8,128)S(1)}) all-reduce(f32[64,64]{1,0:T(8,128)S(1)} %fusion.13, f32[64,64]{1,0:T(8,128)S(1)} %fusion.17, f32[64,64]{1,0:T(8,128)S(1)} %fusion.15), channel_id=1, replica_groups=mesh['groups'=2,'dp'=16] {'dp'}, use_global_device_ids=true, to_apply=%region_7.8 | all-reduce | flops 12288 | bytes 98304 | tf_op jit(solution)/shard_map/psum | solution.py:88
  298.8 5.8 cholesky.70
  306.0 4.9 custom-call.10
  312.1 5.9 cholesky.59
  319.3 4.9 custom-call.9
  326.6 57.6 %psum.63 = f32[64,64]{1,0:T(8,128)S(1)} all-reduce(f32[64,64]{1,0:T(8,128)S(1)} %fusion.63), channel_id=1, replica_groups=mesh['groups'=2,'dp'=16] {'dp'}, use_global_device_ids=true, to_apply=%region_10.13 | all-reduce | flops 4096 | bytes 32768 | tf_op jit(solution)/shard_map/psum | solution.py:106
  385.4 4.4 collective-permute-start.16
  389.8 2.8 collective-permute-done.15
  392.6 4.5 collective-permute-start.18
  397.1 2.7 collective-permute-done.17
  399.8 4.5 collective-permute-start.20
  404.3 2.7 collective-permute-done.19
  407.0 4.5 collective-permute-start.22
  411.5 2.7 collective-permute-done.21
  414.2 4.5 collective-permute-start.24
  418.7 2.7 collective-permute-done.23
  421.4 4.5 collective-permute-start.26
  425.9 2.7 collective-permute-done.25
  428.6 4.5 collective-permute-start.28
  433.1 2.5 collective-permute-done.27
  435.7 7.0 %collective-permute-done.29 = bf16[1024,64]{0,1:T(8,128)(2,1)S(1)} collective-permute-done((bf16[1024,64]{0,1:T(8,128)(2,1)S(1)}, bf16[1024,64]{0,1:T(8,128)(2,1)S(1)}, u32[]{:S(2)}, u32[]{:S(2)}) %collective-permute-start.29) | collective-permute-done | bytes 131104 | tf_op jit(solution)/shard_map/ppermute | solution.py:65
  442.8 17.8 %convolution_bitcast_fusion = f32[16384,64]{0,1:T(8,128)} fusion(bf16[384,16384]{1,0:T(8,128)(2,1)} %param.6, bf16[16384,64]{0,1:T(8,128)(2,1)S(1)} %constant_dynamic-update-slice_fusion, f32[384]{0:T(512)S(1)} %convert_element_type.20), kind=kOutput, calls=%fused_computation | convolution fusion | flops 1610661888 | bytes 18875904 | tf_op jit(solution)/shard_map/dot_general | solution.py:26
  461.9 68.8 %reduce-scatter.8.cloned.1.call-done = f32[1024,64]{0,1:T(8,128)} async-done(((f32[16384,64]{0,1:T(8,128)}), f32[1024,64]{0,1:T(8,128)}) %reduce-scatter.8.cloned.1.call-update) | async-done | bytes 262160 | tf_op jit(solution)/shard_map/reduce_scatter | solution.py:85
  532.0 59.1 %all-reduce = (f32[64,64]{1,0:T(8,128)S(1)}, f32[64,64]{1,0:T(8,128)S(1)}, f32[64,64]{1,0:T(8,128)S(1)}) all-reduce(f32[64,64]{1,0:T(8,128)S(1)} %fusion.64, f32[64,64]{1,0:T(8,128)S(1)} %fusion.61, f32[64,64]{1,0:T(8,128)S(1)} %fusion.65), channel_id=1, replica_groups=mesh['groups'=2,'dp'=16] {'dp'}, use_global_device_ids=true, to_apply=%region_12.15 | all-reduce | flops 12288 | bytes 98304 | tf_op jit(solution)/shard_map/psum | solution.py:88
  592.2 5.8 cholesky.81
  599.4 4.9 custom-call.11
  604.7 2.1 fusion.1
  (123 shorter events, 19.8 us)
Async XLA Ops:
  7.2 84.9 %reduce-scatter.4.cloned.1.call-start = ((), (), s32[]{:S(2)}) async-start(), calls=%async_computation.3 | async-start | bytes 4456448 | tf_op jit(solution)/shard_map/reduce_scatter | solution.py:37
  16.8 0.7 copy-start.1
  16.8 221.2 %reduce-scatter.6.cloned.1.call-start = ((), (), s32[]{:S(2)}) async-start(), calls=%async_computation.4 | async-start | bytes 4456448 | tf_op jit(solution)/shard_map/reduce_scatter | solution.py:85
  92.1 0.9 copy-start
  93.1 7.1 %collective-permute-start = (bf16[1024,64]{0,1:T(8,128)(2,1)S(1)}, bf16[1024,64]{0,1:T(8,128)(2,1)S(1)}, u32[]{:S(2)}, u32[]{:S(2)}) collective-permute-start(bf16[1024,64]{0,1:T(8,128)(2,1)S(1)} %get-tuple-element.13), channel_id=1, source_target_pairs={{0,1},{1,2},{2,3},{3,4},{4,5},{5,6},{6,7},{7,8},{8,9},{9,10},{10,1... | collective-permute-start | bytes 393224 | tf_op jit(solution)/shard_map/ppermute | solution.py:65
  93.2 7.1 %collective-permute-start.1 = (bf16[1024,64]{0,1:T(8,128)(2,1)S(1)}, bf16[1024,64]{0,1:T(8,128)(2,1)S(1)}, u32[]{:S(2)}, u32[]{:S(2)}) collective-permute-start(bf16[1024,64]{0,1:T(8,128)(2,1)S(1)} %get-tuple-element.13), channel_id=1, source_target_pairs={{0,15},{1,0},{2,1},{3,2},{4,3},{5,4},{6,5},{7,6},{8,7},{9,8},{10,9... | collective-permute-start | bytes 393224 | tf_op jit(solution)/shard_map/ppermute | solution.py:70
  100.3 7.2 %collective-permute-start.2 = (bf16[1024,64]{0,1:T(8,128)(2,1)S(1)}, bf16[1024,64]{0,1:T(8,128)(2,1)S(1)}, u32[]{:S(2)}, u32[]{:S(2)}) collective-permute-start(bf16[1024,64]{0,1:T(8,128)(2,1)S(1)} %collective-permute-done), channel_id=1, source_target_pairs={{0,1},{1,2},{2,3},{3,4},{4,5},{5,6},{6,7},{7,8},{8,9},{9,10},{10,1... | collective-permute-start | bytes 393224 | tf_op jit(solution)/shard_map/ppermute | solution.py:65
  100.3 7.2 %collective-permute-start.3 = (bf16[1024,64]{0,1:T(8,128)(2,1)S(1)}, bf16[1024,64]{0,1:T(8,128)(2,1)S(1)}, u32[]{:S(2)}, u32[]{:S(2)}) collective-permute-start(bf16[1024,64]{0,1:T(8,128)(2,1)S(1)} %collective-permute-done.1), channel_id=1, source_target_pairs={{0,15},{1,0},{2,1},{3,2},{4,3},{5,4},{6,5},{7,6},{8,7},{9,8},{10,9... | collective-permute-start | bytes 393224 | tf_op jit(solution)/shard_map/ppermute | solution.py:70
  107.5 7.2 %collective-permute-start.4 = (bf16[1024,64]{0,1:T(8,128)(2,1)S(1)}, bf16[1024,64]{0,1:T(8,128)(2,1)S(1)}, u32[]{:S(2)}, u32[]{:S(2)}) collective-permute-start(bf16[1024,64]{0,1:T(8,128)(2,1)S(1)} %collective-permute-done.2), channel_id=1, source_target_pairs={{0,1},{1,2},{2,3},{3,4},{4,5},{5,6},{6,7},{7,8},{8,9},{9,10},{10,1... | collective-permute-start | bytes 393224 | tf_op jit(solution)/shard_map/ppermute | solution.py:65
  107.5 7.2 %collective-permute-start.5 = (bf16[1024,64]{0,1:T(8,128)(2,1)S(1)}, bf16[1024,64]{0,1:T(8,128)(2,1)S(1)}, u32[]{:S(2)}, u32[]{:S(2)}) collective-permute-start(bf16[1024,64]{0,1:T(8,128)(2,1)S(1)} %collective-permute-done.3), channel_id=1, source_target_pairs={{0,15},{1,0},{2,1},{3,2},{4,3},{5,4},{6,5},{7,6},{8,7},{9,8},{10,9... | collective-permute-start | bytes 393224 | tf_op jit(solution)/shard_map/ppermute | solution.py:70
  114.7 7.2 %collective-permute-start.6 = (bf16[1024,64]{0,1:T(8,128)(2,1)S(1)}, bf16[1024,64]{0,1:T(8,128)(2,1)S(1)}, u32[]{:S(2)}, u32[]{:S(2)}) collective-permute-start(bf16[1024,64]{0,1:T(8,128)(2,1)S(1)} %collective-permute-done.4), channel_id=1, source_target_pairs={{0,1},{1,2},{2,3},{3,4},{4,5},{5,6},{6,7},{7,8},{8,9},{9,10},{10,1... | collective-permute-start | bytes 393224 | tf_op jit(solution)/shard_map/ppermute | solution.py:65
  114.7 7.2 %collective-permute-start.7 = (bf16[1024,64]{0,1:T(8,128)(2,1)S(1)}, bf16[1024,64]{0,1:T(8,128)(2,1)S(1)}, u32[]{:S(2)}, u32[]{:S(2)}) collective-permute-start(bf16[1024,64]{0,1:T(8,128)(2,1)S(1)} %collective-permute-done.5), channel_id=1, source_target_pairs={{0,15},{1,0},{2,1},{3,2},{4,3},{5,4},{6,5},{7,6},{8,7},{9,8},{10,9... | collective-permute-start | bytes 393224 | tf_op jit(solution)/shard_map/ppermute | solution.py:70
  121.9 7.2 %collective-permute-start.8 = (bf16[1024,64]{0,1:T(8,128)(2,1)S(1)}, bf16[1024,64]{0,1:T(8,128)(2,1)S(1)}, u32[]{:S(2)}, u32[]{:S(2)}) collective-permute-start(bf16[1024,64]{0,1:T(8,128)(2,1)S(1)} %collective-permute-done.6), channel_id=1, source_target_pairs={{0,1},{1,2},{2,3},{3,4},{4,5},{5,6},{6,7},{7,8},{8,9},{9,10},{10,1... | collective-permute-start | bytes 393224 | tf_op jit(solution)/shard_map/ppermute | solution.py:65
  121.9 7.2 %collective-permute-start.9 = (bf16[1024,64]{0,1:T(8,128)(2,1)S(1)}, bf16[1024,64]{0,1:T(8,128)(2,1)S(1)}, u32[]{:S(2)}, u32[]{:S(2)}) collective-permute-start(bf16[1024,64]{0,1:T(8,128)(2,1)S(1)} %collective-permute-done.7), channel_id=1, source_target_pairs={{0,15},{1,0},{2,1},{3,2},{4,3},{5,4},{6,5},{7,6},{8,7},{9,8},{10,9... | collective-permute-start | bytes 393224 | tf_op jit(solution)/shard_map/ppermute | solution.py:70
  129.1 7.2 %collective-permute-start.10 = (bf16[1024,64]{0,1:T(8,128)(2,1)S(1)}, bf16[1024,64]{0,1:T(8,128)(2,1)S(1)}, u32[]{:S(2)}, u32[]{:S(2)}) collective-permute-start(bf16[1024,64]{0,1:T(8,128)(2,1)S(1)} %collective-permute-done.8), channel_id=1, source_target_pairs={{0,1},{1,2},{2,3},{3,4},{4,5},{5,6},{6,7},{7,8},{8,9},{9,10},{10,1... | collective-permute-start | bytes 393224 | tf_op jit(solution)/shard_map/ppermute | solution.py:65
  129.1 7.2 %collective-permute-start.11 = (bf16[1024,64]{0,1:T(8,128)(2,1)S(1)}, bf16[1024,64]{0,1:T(8,128)(2,1)S(1)}, u32[]{:S(2)}, u32[]{:S(2)}) collective-permute-start(bf16[1024,64]{0,1:T(8,128)(2,1)S(1)} %collective-permute-done.9), channel_id=1, source_target_pairs={{0,15},{1,0},{2,1},{3,2},{4,3},{5,4},{6,5},{7,6},{8,7},{9,8},{10,9... | collective-permute-start | bytes 393224 | tf_op jit(solution)/shard_map/ppermute | solution.py:70
  136.3 7.1 %collective-permute-start.12 = (bf16[1024,64]{0,1:T(8,128)(2,1)S(1)}, bf16[1024,64]{0,1:T(8,128)(2,1)S(1)}, u32[]{:S(2)}, u32[]{:S(2)}) collective-permute-start(bf16[1024,64]{0,1:T(8,128)(2,1)S(1)} %collective-permute-done.10), channel_id=1, source_target_pairs={{0,1},{1,2},{2,3},{3,4},{4,5},{5,6},{6,7},{7,8},{8,9},{9,10},{10,1... | collective-permute-start | bytes 393224 | tf_op jit(solution)/shard_map/ppermute | solution.py:65
  136.3 7.1 %collective-permute-start.13 = (bf16[1024,64]{0,1:T(8,128)(2,1)S(1)}, bf16[1024,64]{0,1:T(8,128)(2,1)S(1)}, u32[]{:S(2)}, u32[]{:S(2)}) collective-permute-start(bf16[1024,64]{0,1:T(8,128)(2,1)S(1)} %collective-permute-done.11), channel_id=1, source_target_pairs={{0,15},{1,0},{2,1},{3,2},{4,3},{5,4},{6,5},{7,6},{8,7},{9,8},{10,9... | collective-permute-start | bytes 393224 | tf_op jit(solution)/shard_map/ppermute | solution.py:70
  143.3 7.1 %collective-permute-start.14 = (bf16[1024,64]{0,1:T(8,128)(2,1)S(1)}, bf16[1024,64]{0,1:T(8,128)(2,1)S(1)}, u32[]{:S(2)}, u32[]{:S(2)}) collective-permute-start(bf16[1024,64]{0,1:T(8,128)(2,1)S(1)} %collective-permute-done.12), channel_id=1, source_target_pairs={{0,1},{1,2},{2,3},{3,4},{4,5},{5,6},{6,7},{7,8},{8,9},{9,10},{10,1... | collective-permute-start | bytes 393224 | tf_op jit(solution)/shard_map/ppermute | solution.py:65
  168.3 362.4 %reduce-scatter.8.cloned.1.call-start = ((), (), s32[]{:S(2)}) async-start(), calls=%async_computation.5 | async-start | bytes 4456448 | tf_op jit(solution)/shard_map/reduce_scatter | solution.py:85
  238.0 86.6 %copy-start.2 = (f32[1024,64]{0,1:T(8,128)S(1)}, f32[1024,64]{0,1:T(8,128)}, u32[]{:S(2)}) copy-start(f32[1024,64]{0,1:T(8,128)} %reduce-scatter.6.cloned.1.call-done) | copy-start | bytes 786436
  385.3 7.2 %collective-permute-start.15 = (bf16[1024,64]{0,1:T(8,128)(2,1)S(1)}, bf16[1024,64]{0,1:T(8,128)(2,1)S(1)}, u32[]{:S(2)}, u32[]{:S(2)}) collective-permute-start(bf16[1024,64]{0,1:T(8,128)(2,1)S(1)} %get-tuple-element.11), channel_id=1, source_target_pairs={{0,1},{1,2},{2,3},{3,4},{4,5},{5,6},{6,7},{7,8},{8,9},{9,10},{10,1... | collective-permute-start | bytes 393224 | tf_op jit(solution)/shard_map/ppermute | solution.py:65
  385.4 7.2 %collective-permute-start.16 = (bf16[1024,64]{0,1:T(8,128)(2,1)S(1)}, bf16[1024,64]{0,1:T(8,128)(2,1)S(1)}, u32[]{:S(2)}, u32[]{:S(2)}) collective-permute-start(bf16[1024,64]{0,1:T(8,128)(2,1)S(1)} %get-tuple-element.11), channel_id=1, source_target_pairs={{0,15},{1,0},{2,1},{3,2},{4,3},{5,4},{6,5},{7,6},{8,7},{9,8},{10,9... | collective-permute-start | bytes 393224 | tf_op jit(solution)/shard_map/ppermute | solution.py:70
  392.6 7.2 %collective-permute-start.17 = (bf16[1024,64]{0,1:T(8,128)(2,1)S(1)}, bf16[1024,64]{0,1:T(8,128)(2,1)S(1)}, u32[]{:S(2)}, u32[]{:S(2)}) collective-permute-start(bf16[1024,64]{0,1:T(8,128)(2,1)S(1)} %collective-permute-done.15), channel_id=1, source_target_pairs={{0,1},{1,2},{2,3},{3,4},{4,5},{5,6},{6,7},{7,8},{8,9},{9,10},{10,1... | collective-permute-start | bytes 393224 | tf_op jit(solution)/shard_map/ppermute | solution.py:65
  392.6 7.2 %collective-permute-start.18 = (bf16[1024,64]{0,1:T(8,128)(2,1)S(1)}, bf16[1024,64]{0,1:T(8,128)(2,1)S(1)}, u32[]{:S(2)}, u32[]{:S(2)}) collective-permute-start(bf16[1024,64]{0,1:T(8,128)(2,1)S(1)} %collective-permute-done.16), channel_id=1, source_target_pairs={{0,15},{1,0},{2,1},{3,2},{4,3},{5,4},{6,5},{7,6},{8,7},{9,8},{10,9... | collective-permute-start | bytes 393224 | tf_op jit(solution)/shard_map/ppermute | solution.py:70
  399.8 7.2 %collective-permute-start.19 = (bf16[1024,64]{0,1:T(8,128)(2,1)S(1)}, bf16[1024,64]{0,1:T(8,128)(2,1)S(1)}, u32[]{:S(2)}, u32[]{:S(2)}) collective-permute-start(bf16[1024,64]{0,1:T(8,128)(2,1)S(1)} %collective-permute-done.17), channel_id=1, source_target_pairs={{0,1},{1,2},{2,3},{3,4},{4,5},{5,6},{6,7},{7,8},{8,9},{9,10},{10,1... | collective-permute-start | bytes 393224 | tf_op jit(solution)/shard_map/ppermute | solution.py:65
  399.8 7.2 %collective-permute-start.20 = (bf16[1024,64]{0,1:T(8,128)(2,1)S(1)}, bf16[1024,64]{0,1:T(8,128)(2,1)S(1)}, u32[]{:S(2)}, u32[]{:S(2)}) collective-permute-start(bf16[1024,64]{0,1:T(8,128)(2,1)S(1)} %collective-permute-done.18), channel_id=1, source_target_pairs={{0,15},{1,0},{2,1},{3,2},{4,3},{5,4},{6,5},{7,6},{8,7},{9,8},{10,9... | collective-permute-start | bytes 393224 | tf_op jit(solution)/shard_map/ppermute | solution.py:70
  407.0 7.2 %collective-permute-start.21 = (bf16[1024,64]{0,1:T(8,128)(2,1)S(1)}, bf16[1024,64]{0,1:T(8,128)(2,1)S(1)}, u32[]{:S(2)}, u32[]{:S(2)}) collective-permute-start(bf16[1024,64]{0,1:T(8,128)(2,1)S(1)} %collective-permute-done.19), channel_id=1, source_target_pairs={{0,1},{1,2},{2,3},{3,4},{4,5},{5,6},{6,7},{7,8},{8,9},{9,10},{10,1... | collective-permute-start | bytes 393224 | tf_op jit(solution)/shard_map/ppermute | solution.py:65
  407.0 7.2 %collective-permute-start.22 = (bf16[1024,64]{0,1:T(8,128)(2,1)S(1)}, bf16[1024,64]{0,1:T(8,128)(2,1)S(1)}, u32[]{:S(2)}, u32[]{:S(2)}) collective-permute-start(bf16[1024,64]{0,1:T(8,128)(2,1)S(1)} %collective-permute-done.20), channel_id=1, source_target_pairs={{0,15},{1,0},{2,1},{3,2},{4,3},{5,4},{6,5},{7,6},{8,7},{9,8},{10,9... | collective-permute-start | bytes 393224 | tf_op jit(solution)/shard_map/ppermute | solution.py:70
  414.2 7.2 %collective-permute-start.23 = (bf16[1024,64]{0,1:T(8,128)(2,1)S(1)}, bf16[1024,64]{0,1:T(8,128)(2,1)S(1)}, u32[]{:S(2)}, u32[]{:S(2)}) collective-permute-start(bf16[1024,64]{0,1:T(8,128)(2,1)S(1)} %collective-permute-done.21), channel_id=1, source_target_pairs={{0,1},{1,2},{2,3},{3,4},{4,5},{5,6},{6,7},{7,8},{8,9},{9,10},{10,1... | collective-permute-start | bytes 393224 | tf_op jit(solution)/shard_map/ppermute | solution.py:65
  414.2 7.2 %collective-permute-start.24 = (bf16[1024,64]{0,1:T(8,128)(2,1)S(1)}, bf16[1024,64]{0,1:T(8,128)(2,1)S(1)}, u32[]{:S(2)}, u32[]{:S(2)}) collective-permute-start(bf16[1024,64]{0,1:T(8,128)(2,1)S(1)} %collective-permute-done.22), channel_id=1, source_target_pairs={{0,15},{1,0},{2,1},{3,2},{4,3},{5,4},{6,5},{7,6},{8,7},{9,8},{10,9... | collective-permute-start | bytes 393224 | tf_op jit(solution)/shard_map/ppermute | solution.py:70
  421.4 7.2 %collective-permute-start.25 = (bf16[1024,64]{0,1:T(8,128)(2,1)S(1)}, bf16[1024,64]{0,1:T(8,128)(2,1)S(1)}, u32[]{:S(2)}, u32[]{:S(2)}) collective-permute-start(bf16[1024,64]{0,1:T(8,128)(2,1)S(1)} %collective-permute-done.23), channel_id=1, source_target_pairs={{0,1},{1,2},{2,3},{3,4},{4,5},{5,6},{6,7},{7,8},{8,9},{9,10},{10,1... | collective-permute-start | bytes 393224 | tf_op jit(solution)/shard_map/ppermute | solution.py:65
  421.4 7.2 %collective-permute-start.26 = (bf16[1024,64]{0,1:T(8,128)(2,1)S(1)}, bf16[1024,64]{0,1:T(8,128)(2,1)S(1)}, u32[]{:S(2)}, u32[]{:S(2)}) collective-permute-start(bf16[1024,64]{0,1:T(8,128)(2,1)S(1)} %collective-permute-done.24), channel_id=1, source_target_pairs={{0,15},{1,0},{2,1},{3,2},{4,3},{5,4},{6,5},{7,6},{8,7},{9,8},{10,9... | collective-permute-start | bytes 393224 | tf_op jit(solution)/shard_map/ppermute | solution.py:70
  428.6 7.1 %collective-permute-start.27 = (bf16[1024,64]{0,1:T(8,128)(2,1)S(1)}, bf16[1024,64]{0,1:T(8,128)(2,1)S(1)}, u32[]{:S(2)}, u32[]{:S(2)}) collective-permute-start(bf16[1024,64]{0,1:T(8,128)(2,1)S(1)} %collective-permute-done.25), channel_id=1, source_target_pairs={{0,1},{1,2},{2,3},{3,4},{4,5},{5,6},{6,7},{7,8},{8,9},{9,10},{10,1... | collective-permute-start | bytes 393224 | tf_op jit(solution)/shard_map/ppermute | solution.py:65
  428.6 7.1 %collective-permute-start.28 = (bf16[1024,64]{0,1:T(8,128)(2,1)S(1)}, bf16[1024,64]{0,1:T(8,128)(2,1)S(1)}, u32[]{:S(2)}, u32[]{:S(2)}) collective-permute-start(bf16[1024,64]{0,1:T(8,128)(2,1)S(1)} %collective-permute-done.26), channel_id=1, source_target_pairs={{0,15},{1,0},{2,1},{3,2},{4,3},{5,4},{6,5},{7,6},{8,7},{9,8},{10,9... | collective-permute-start | bytes 393224 | tf_op jit(solution)/shard_map/ppermute | solution.py:70
  435.7 7.1 %collective-permute-start.29 = (bf16[1024,64]{0,1:T(8,128)(2,1)S(1)}, bf16[1024,64]{0,1:T(8,128)(2,1)S(1)}, u32[]{:S(2)}, u32[]{:S(2)}) collective-permute-start(bf16[1024,64]{0,1:T(8,128)(2,1)S(1)} %collective-permute-done.27), channel_id=1, source_target_pairs={{0,1},{1,2},{2,3},{3,4},{4,5},{5,6},{6,7},{7,8},{8,9},{9,10},{10,1... | collective-permute-start | bytes 393224 | tf_op jit(solution)/shard_map/ppermute | solution.py:65
Sparse Core Ops, SparseCore 0:
  16.9 75.1 reduce-scatter.3
  168.4 69.5 reduce-scatter.5
  460.7 69.8 reduce-scatter.7
